TPU v7x, 256 devices: a whole 4x4x8 slice. The times are simulated.
256 devices in a mesh: dp: 4 (over x), expert: 64 (over y, z, core).
Axes of the slice: x: 4, y: 4, z: 8, core: 2. Of those that a mesh axis runs over, the one named last changes fastest.
Arguments:
- tokens: bfloat16 [4096, 3584], P(('dp', 'expert')), may hold values from -6 to 6
- out_grad: bfloat16 [4096, 3584], P(('dp', 'expert')), may hold values from -6 to 6
- route_ids: int32 [4096, 8], P(('dp', 'expert')), may hold values from 0 to 127, all different within a row; in each aligned block of 16 rows (0 to 15, 16 to 31, ...) at most 2 rows name the same one
- route_probs: float32 [4096, 8], P(('dp', 'expert')), may hold values from 0.02 to 0.5
- w_gate: bfloat16 [128, 3584, 1024], P('expert', None, 'dp'), may hold values from -0.09375 to 0.09375
- w_up: bfloat16 [128, 3584, 1024], P('expert', None, 'dp'), may hold values from -0.09375 to 0.09375
- w_down: bfloat16 [128, 1024, 3584], P('expert', 'dp'), may hold values from -0.1875 to 0.1875
Outputs:
- in_grad: bfloat16 [4096, 3584], P(('dp', 'expert'))
Inputs may be any that keep to these rules, and one draw needn't show every extreme that they name: `route_ids`: the 8 ids of a token differ. Among the tokens of one device (aligned blocks of 16 rows) no expert is named more than 2 times, and in every draw some expert is named exactly 2 times there.
All inputs are finite; a program needn't handle non-finite values.
Results may differ from a plain program's by a relative error of at most 0.015.
Values may be sent and summed in bfloat16 or wider, within the bound.
No kernel may reach another device: no remote copies, remote signals or barrier semaphores. Data moves between devices by JAX's collectives and lax.ppermute only.
A program may use at most 128 MiB of HBM per device.

v0:
```python
import jax
import jax.numpy as jnp
from jax import lax
from jax.sharding import PartitionSpec as P

TOPK = 8


def slot_matches(flat_ids, experts, capacity):
    onehot = (flat_ids[:, None] == jnp.arange(experts, dtype=jnp.int32)[None, :]).astype(jnp.int32)
    earlier = jnp.cumsum(onehot, axis=0) - onehot
    slot_rank = jnp.sum(earlier * onehot, axis=1)
    slot_of = flat_ids * capacity + slot_rank
    return slot_of[None, :] == jnp.arange(experts * capacity, dtype=jnp.int32)[:, None]


def select_matrix(matches, tok_count):
    return jnp.sum(matches.reshape(matches.shape[0], tok_count, TOPK).astype(jnp.float32), axis=2)


def build_tiles(token_rows, grad_rows, matches, flat_probs):
    select = select_matrix(matches, token_rows.shape[0]).astype(jnp.bfloat16)
    slot_scale = jnp.sum(jnp.where(matches, flat_probs[None, :], 0.0), axis=1)
    x_rows = jnp.dot(select, token_rows, preferred_element_type=jnp.float32).astype(jnp.bfloat16)
    g_rows = (
        jnp.dot(select, grad_rows, preferred_element_type=jnp.float32) * slot_scale[:, None]
    ).astype(jnp.bfloat16)
    return jnp.stack([x_rows, g_rows])


def expert_grads(tiles, w_gate, w_up, w_down):
    x_rows = tiles[:, 0]
    g_rows = tiles[:, 1]
    gate_pre = jnp.einsum("nsecd,edh->nsech", x_rows, w_gate, preferred_element_type=jnp.float32)
    up_pre = jnp.einsum("nsecd,edh->nsech", x_rows, w_up, preferred_element_type=jnp.float32)
    hidden_grad = jnp.einsum("nsecd,ehd->nsech", g_rows, w_down, preferred_element_type=jnp.float32)
    sigmoid_a = jax.nn.sigmoid(gate_pre)
    gate_grad = (hidden_grad * up_pre * sigmoid_a * (1.0 + gate_pre * (1.0 - sigmoid_a))).astype(
        jnp.bfloat16
    )
    up_grad = (hidden_grad * gate_pre * sigmoid_a).astype(jnp.bfloat16)
    partial_value = jnp.einsum(
        "nsech,edh->nsecd", gate_grad, w_gate, preferred_element_type=jnp.float32
    )
    partial_value = partial_value + jnp.einsum(
        "nsech,edh->nsecd", up_grad, w_up, preferred_element_type=jnp.float32
    )
    return partial_value.astype(jnp.bfloat16)


def on_device(tokens, out_grad, route_ids, route_probs, w_gate, w_up, w_down):
    columns = lax.axis_size("expert")
    local_experts = w_gate.shape[0]
    experts = local_experts * columns
    tok_count, width = tokens.shape
    capacity = max(2, 2 * tok_count * TOPK // experts)
    slots = experts * capacity
    tile_shape = (2, columns, local_experts, capacity, width)
    own_matches = slot_matches(route_ids.reshape(-1), experts, capacity)
    tiles = build_tiles(tokens, out_grad, own_matches, route_probs.reshape(-1)).reshape(
        (1,) + tile_shape
    )
    received = lax.all_to_all(tiles, "expert", split_axis=2, concat_axis=2, tiled=True)
    partials = expert_grads(
        lax.all_gather(received, "dp", axis=0, tiled=True), w_gate, w_up, w_down
    )
    summed = lax.psum_scatter(
        partials.astype(jnp.float32).astype(jnp.bfloat16), "dp", scatter_dimension=0, tiled=True
    ).astype(jnp.float32)
    returned = lax.all_to_all(
        summed.astype(jnp.bfloat16), "expert", split_axis=1, concat_axis=1, tiled=True
    ).astype(summed.dtype)
    own_select = select_matrix(own_matches, tok_count)
    result = jnp.dot(own_select.T, returned.reshape(slots, width), precision=lax.Precision.HIGHEST)
    return result.astype(jnp.bfloat16)


def solution(mesh):
    placed = (
        P(("dp", "expert"), None),
        P(("dp", "expert"), None),
        P(("dp", "expert"), None),
        P(("dp", "expert"), None),
        P("expert", None, "dp"),
        P("expert", None, "dp"),
        P("expert", "dp", None),
    )
    return jax.shard_map(
        on_device, mesh=mesh, in_specs=placed, out_specs=P(("dp", "expert"), None), check_vma=False
    )
```

profile of v0, /device:TPU:1, one launch (start us, length us, event | category | flops | bytes accessed | tf_op | source)
XLA Modules:
  0.0 523.0 jit_solution(11787229914710495954)
XLA Ops:
  6.5 0.8 copy.26
  8.1 0.8 copy.28
  9.1 1.9 fusion.4
  11.0 3.9 stack.10
  14.9 1.9 convolution_convert_fusion
  16.8 4.7 stack.9
  21.6 6.4 %pad_maximum_fusion = bf16[1,2,64,2,2,3584]{5,4,0,3,1,2:T(2,128)(2,1)S(1)} fusion(bf16[1,1,64,2,2,3584]{5,4,0,3,1,2:T(2,128)(2,1)S(1)} %bitcast.88, bf16[1,1,64,2,2,3584]{5,4,0,3,1,2:T(2,128)(2,1)} %bitcast.89), kind=kLoop, calls=%fused_computation.11 | loop fusion | flops 1835008 | bytes 7340032 | tf_op jit(solution)/shard_map/stack | solution.py:28
  28.0 97.7 %all_to_all.10 = bf16[1,2,64,2,2,3584]{5,4,0,3,1,2:T(2,128)(2,1)S(1)} all-to-all(bf16[1,2,64,2,2,3584]{5,4,0,3,1,2:T(2,128)(2,1)S(1)} %pad_maximum_fusion), channel_id=1, replica_groups=mesh['dp'=4,'expert'=64] {'expert'}, dimensions={2} | all-to-all | bytes 7340032 | tf_op jit(solution)/shard_map/all_to_all | solution.py:63
  125.7 2.9 copy.31
  128.8 135.5 %all-gather.2.cloned.1.call-done = bf16[4,2,64,2,2,3584]{5,2,4,0,3,1:T(8,128)(2,1)} async-done(((bf16[1,2,64,2,2,3584]{5,2,4,0,3,1:T(8,128)(2,1)}), bf16[4,2,64,2,2,3584]{5,2,4,0,3,1:T(8,128)(2,1)}) %all-gather.2.cloned.1.call-update) | async-done | bytes 14680080 | tf_op jit(solution)/shard_map/all_gather | solution.py:65
  264.3 6.3 %fusion.14 = f32[4,64,2,2,256]{4,1,3,0,2:T(8,128)S(1)} fusion(bf16[2,3584,256]{2,1,0:T(8,128)(2,1)} %param.11, bf16[4,2,64,2,2,3584]{5,2,4,0,3,1:T(8,128)(2,1)} %all-gather.2.cloned.1.call-done), kind=kOutput, calls=%fused_computation.19 | convolution fusion | flops 1879048192 | bytes 12058624 | tf_op jit(solution)/shard_map/nsecd,edh->nsech/dot_general | solution.py:34
  270.7 2.0 copy-done.5
  272.6 4.3 fusion.17
  276.9 5.5 %fusion.29 = bf16[4,64,2,2,256]{4,1,3,0,2:T(8,128)(2,1)S(1)} fusion(f32[4,64,2,2,256]{4,1,3,0,2:T(8,128)S(1)} %fusion.17, bf16[2,3584,256]{2,1,0:T(8,128)(2,1)S(1)} %copy-done.3, bf16[4,2,64,2,2,3584]{5,2,4,0,3,1:T(8,128)(2,1)} %all-gather.2.cloned.1.call-done, f32[4,64,2,2,256]{4,1,3,0,2:T(8,128)S(1)} %fusion.14), kind=kOutput, calls=%fused_computation.24 | convolution fusion | flops 1881669632 | bytes 13631488 | tf_op jit(solution)/shard_map/nsecd,edh->nsech/dot_general | solution.py:35
  282.4 7.3 %fusion.5 = f32[2,4,64,2,3584]{4,2,3,1,0:T(8,128)} fusion(bf16[4,64,2,2,256]{4,1,3,0,2:T(8,128)(2,1)S(1)} %fusion.29, bf16[2,3584,256]{2,1,0:T(8,128)(2,1)S(1)} %copy-done.2), kind=kOutput, calls=%fused_computation.12 | convolution fusion | flops 1879048192 | bytes 18874368 | tf_op jit(solution)/shard_map/nsech,edh->nsecd/dot_general | solution.py:42
  289.8 11.3 %fusion.1 = bf16[4,64,2,2,3584]{4,1,3,0,2:T(8,128)(2,1)} fusion(f32[2,4,64,2,3584]{4,2,3,1,0:T(8,128)} %fusion.5, bf16[2,3584,256]{2,1,0:T(8,128)(2,1)} %param.12, f32[4,64,2,2,256]{4,1,3,0,2:T(8,128)S(1)} %fusion.17, f32[4,64,2,2,256]{4,1,3,0,2:T(8,128)S(1)} %fusion.14), kind=kOutput, calls=%fused_computation.4 | convolution fusion | flops 1887961088 | bytes 27787264 | tf_op jit(solution)/shard_map/nsech,edh->nsecd/dot_general | solution.py:45
  301.1 0.6 copy-done.6
  301.8 0.6 dynamic-slice
  302.4 148.9 %all-reduce.3.cloned.1.call-done = bf16[4,64,2,2,3584]{4,1,3,0,2:T(8,128)(2,1)} async-done(((bf16[4,64,2,2,3584]{4,1,3,0,2:T(8,128)(2,1)}), bf16[4,64,2,2,3584]{4,1,3,0,2:T(8,128)(2,1)}) %all-reduce.3.cloned.1.call-update) | async-done | bytes 7340048
  451.3 2.3 constant_dynamic-slice_fusion
  453.6 1.9 copy.32
  455.5 56.1 %all_to_all.11 = bf16[1,64,2,2,3584]{4,3,0,2,1:T(2,128)(2,1)S(1)} all-to-all(bf16[1,64,2,2,3584]{4,3,0,2,1:T(2,128)(2,1)S(1)} %copy.32), channel_id=1, replica_groups=mesh['dp'=4,'expert'=64] {'expert'}, dimensions={1} | all-to-all | bytes 3670016 | tf_op jit(solution)/shard_map/all_to_all | solution.py:70
  511.6 1.7 reshape.31
  513.2 3.0 convolution_convert_fusion.1
  (26 shorter events, 1.2 us)
Async XLA Ops:
  6.5 2.5 copy-start
  6.5 8.4 %copy-start.4 = (bf16[16,3584]{1,0:T(8,128)(2,1)S(1)}, bf16[16,3584]{1,0:T(8,128)(2,1)}, u32[]{:S(2)}) copy-start(bf16[16,3584]{1,0:T(8,128)(2,1)} %param.7) | copy-start | bytes 344068
  6.5 257.8 %all-gather.2.cloned.1.call-start = ((), (), s32[]{:S(2)}) async-start(), calls=%async_computation.2 | async-start | bytes 18350080 | tf_op jit(solution)/shard_map/all_gather | solution.py:65
  128.6 322.8 %all-reduce.3.cloned.1.call-start = ((), (), s32[]{:S(2)}) async-start(), calls=%async_computation.3 | async-start | bytes 14680064
  264.3 8.3 %copy-start.5 = (bf16[4,2,64,2,2,3584]{5,2,4,0,3,1:T(8,128)(2,1)S(1)}, bf16[4,2,64,2,2,3584]{5,2,4,0,3,1:T(8,128)(2,1)}, u32[]{:S(2)}) copy-start(bf16[4,2,64,2,2,3584]{5,2,4,0,3,1:T(8,128)(2,1)} %all-gather.2.cloned.1.call-done) | copy-start | bytes 44040196
  272.6 4.3 copy-start.3
  276.9 5.5 %copy-start.2 = (bf16[2,3584,256]{2,1,0:T(8,128)(2,1)S(1)}, bf16[2,3584,256]{2,1,0:T(8,128)(2,1)}, u32[]{:S(2)}) copy-start(bf16[2,3584,256]{2,1,0:T(8,128)(2,1)} %param.11) | copy-start | bytes 11010052
  301.1 0.7 copy-start.6
  455.5 60.7 %copy-start.1 = (bf16[16,3584]{1,0:T(8,128)(2,1)S(1)}, bf16[16,3584]{1,0:T(8,128)(2,1)}, u32[]{:S(2)}) copy-start(bf16[16,3584]{1,0:T(8,128)(2,1)} %param.8) | copy-start | bytes 344068
Sparse Core Ops, SparseCore 0:
  128.7 135.6 all-gather.1
  301.2 150.0 all-reduce.2
where the time goes:
time: 523 us
  waiting for transfers between devices  285 us (54%)
  blocking collectives  154 us (29%)
  matrix products  41.6 us (8%)
  local copies, waits for them, and re-layouts  22.3 us (4%)
  between operations  13.5 us (3%)
  other arithmetic  7.1 us (1%)
    unnamed x3, waiting for transfers between devices  149 us
    all_gather x1, waiting for transfers between devices, on_device(): lax.all_gather(received, 'dp', axis=0, tiled=True)  136 us
    all_to_all x1, blocking collectives, on_device(): lax.all_to_all(tiles, 'expert', split_axis=2, concat_axis=2, tiled=True)  97.7 us
    all_to_all x1, blocking collectives, on_device(): lax.all_to_all(summed.astype(jnp.bfloat16), 'expert', split_axis=1, conca...  56.1 us
    dot_general x1, matrix products, expert_grads(): jnp.einsum('nsech,edh->nsecd', up_grad, w_up, preferred_element_type=jnp....  11.3 us
  transfers between devices with their start and end apart: 2, of which 2 were waited for; matrix products, arithmetic and copies ran while one was open for 0% of the time, Pallas kernels for 0%

commit v1 on v0

--- a/solution.py
+++ b/solution.py
@@ -4,6 +4,18 @@
 from jax.sharding import PartitionSpec as P
 
 TOPK = 8
+
+
+def leaf_wait(along_axis, array_here, row_dim):
+    return jnp.concatenate(
+        lax.all_to_all(
+            jnp.stack([array_here] * lax.axis_size(along_axis), axis=0),
+            axis_name=along_axis,
+            split_axis=0,
+            concat_axis=0,
+        ),
+        axis=row_dim,
+    )
 
 
 def slot_matches(flat_ids, experts, capacity):
@@ -61,9 +73,7 @@
         (1,) + tile_shape
     )
     received = lax.all_to_all(tiles, "expert", split_axis=2, concat_axis=2, tiled=True)
-    partials = expert_grads(
-        lax.all_gather(received, "dp", axis=0, tiled=True), w_gate, w_up, w_down
-    )
+    partials = expert_grads(leaf_wait("dp", received, 0), w_gate, w_up, w_down)
     summed = lax.psum_scatter(
         partials.astype(jnp.float32).astype(jnp.bfloat16), "dp", scatter_dimension=0, tiled=True
     ).astype(jnp.float32)

time: 523 us -> 544 us (1.040)
  blocking collectives: 154 us -> 318 us
  waiting for transfers between devices: 285 us -> 144 us
    all_to_all x0 -> x1, blocking collectives: none -> 165 us  [leaf_wait(): lax.all_to_all(jnp.stack([array_here] * lax.axis_size(along_axis), axis=0...]
    all_gather x1 -> x0, waiting for transfers between devices: 136 us -> none  [on_device(): lax.all_gather(received, 'dp', axis=0, tiled=True)]
    unnamed x3 -> x2, waiting for transfers between devices: 149 us -> 144 us
  transfers between devices with their start and end apart: 2 -> 1, of which waited for: 2 -> 1; matrix products, arithmetic and copies ran while one was open for 0% -> 0% of each run, Pallas kernels for 0% -> 0%
where the time goes in v1:
time: 544 us; the launch traced here: 543 us
  blocking collectives  318 us (58%)
  waiting for transfers between devices  144 us (26%)
  matrix products  37.6 us (7%)
  local copies, waits for them, and re-layouts  22.9 us (4%)
  between operations  13.5 us (2%)
  other arithmetic  7.1 us (1%)
    all_to_all x1, blocking collectives, leaf_wait(): lax.all_to_all(jnp.stack([array_here] * lax.axis_size(along_axis), axis=0...  165 us
    unnamed x2, waiting for transfers between devices  144 us
    all_to_all x1, blocking collectives, on_device(): lax.all_to_all(tiles, 'expert', split_axis=2, concat_axis=2, tiled=True)  97.7 us
    all_to_all x1, blocking collectives, on_device(): lax.all_to_all(summed.astype(jnp.bfloat16), 'expert', split_axis=1, conca...  56.1 us
    dot_general x1, matrix products, expert_grads(): jnp.einsum('nsech,edh->nsecd', up_grad, w_up, preferred_element_type=jnp....  11.4 us
  transfers between devices with their start and end apart: 1, of which 1 were waited for; matrix products, arithmetic and copies ran while one was open for 0% of the time, Pallas kernels for 0%

profile of v1, /device:TPU:1, one launch (start us, length us, event | category | flops | bytes accessed | tf_op | source)
XLA Modules:
  0.0 543.2 jit_solution(14633718708053179238)
XLA Ops:
  6.5 0.8 copy.25
  8.1 0.8 copy.27
  9.1 1.9 fusion.4
  11.0 3.9 stack.17
  14.9 1.9 convolution_convert_fusion
  16.8 4.7 stack.16
  21.6 6.4 %pad_maximum_fusion = bf16[1,2,64,2,2,3584]{5,4,3,1,0,2:T(2,128)(2,1)S(1)} fusion(bf16[1,1,64,2,2,3584]{5,4,3,1,0,2:T(2,128)(2,1)S(1)} %bitcast.96, bf16[1,1,64,2,2,3584]{5,4,3,1,0,2:T(2,128)(2,1)} %bitcast.97), kind=kLoop, calls=%fused_computation.12 | loop fusion | flops 1835008 | bytes 7340032 | tf_op jit(solution)/shard_map/stack | solution.py:40
  28.0 97.7 %all_to_all.18 = bf16[1,2,64,2,2,3584]{5,4,3,1,0,2:T(2,128)(2,1)S(1)} all-to-all(bf16[1,2,64,2,2,3584]{5,4,3,1,0,2:T(2,128)(2,1)S(1)} %pad_maximum_fusion), channel_id=1, replica_groups=mesh['dp'=4,'expert'=64] {'expert'}, dimensions={2} | all-to-all | bytes 7340032 | tf_op jit(solution)/shard_map/all_to_all | solution.py:75
  125.7 1.1 copy.30
  126.7 1.8 stack.19
  128.5 164.6 %all_to_all.19 = bf16[4,1,2,64,2,2,3584]{6,3,5,4,2,1,0:T(8,128)(2,1)S(1)} all-to-all(bf16[4,1,2,64,2,2,3584]{6,3,5,4,2,1,0:T(8,128)(2,1)S(1)} %stack.19), channel_id=1, replica_groups=mesh['dp'=4,'expert'=64] {'dp'}, dimensions={0} | all-to-all | bytes 29360128 | tf_op jit(solution)/shard_map/all_to_all | solution.py:11
  293.2 2.6 copy.39
  295.8 3.1 fusion.14
  298.8 5.3 fusion.17
  304.1 3.8 fusion.29
  307.9 7.3 %fusion.5 = f32[2,4,64,2,3584]{4,2,3,1,0:T(8,128)} fusion(bf16[4,64,2,2,256]{4,1,3,0,2:T(8,128)(2,1)S(1)} %fusion.29, bf16[2,3584,256]{2,1,0:T(8,128)(2,1)S(1)} %copy-done.2), kind=kOutput, calls=%fused_computation.13 | convolution fusion | flops 1879048192 | bytes 18874368 | tf_op jit(solution)/shard_map/nsech,edh->nsecd/dot_general | solution.py:54
  315.2 11.4 %fusion.1 = bf16[4,64,2,2,3584]{4,1,3,0,2:T(8,128)(2,1)} fusion(f32[2,4,64,2,3584]{4,2,3,1,0:T(8,128)} %fusion.5, bf16[2,3584,256]{2,1,0:T(8,128)(2,1)} %param.12, f32[4,64,2,2,256]{4,1,3,0,2:T(8,128)S(1)} %copy-done.5, f32[4,64,2,2,256]{4,1,3,0,2:T(8,128)S(1)} %copy-done.4), kind=kOutput, calls=%fused_computation.5 | convolution fusion | flops 1887961088 | bytes 27787264 | tf_op jit(solution)/shard_map/nsech,edh->nsecd/dot_general | solution.py:57
  326.6 0.6 copy-done.7
  327.8 143.6 %all-reduce.3.cloned.1.call-done = bf16[4,64,2,2,3584]{4,1,3,0,2:T(8,128)(2,1)} async-done(((bf16[4,64,2,2,3584]{4,1,3,0,2:T(8,128)(2,1)}), bf16[4,64,2,2,3584]{4,1,3,0,2:T(8,128)(2,1)}) %all-reduce.3.cloned.1.call-update) | async-done | bytes 7340048
  471.5 2.3 constant_dynamic-slice_fusion
  473.7 1.9 copy.32
  475.6 56.1 %all_to_all.20 = bf16[1,64,2,2,3584]{4,3,0,2,1:T(2,128)(2,1)S(1)} all-to-all(bf16[1,64,2,2,3584]{4,3,0,2,1:T(2,128)(2,1)S(1)} %copy.32), channel_id=1, replica_groups=mesh['dp'=4,'expert'=64] {'expert'}, dimensions={1} | all-to-all | bytes 3670016 | tf_op jit(solution)/shard_map/all_to_all | solution.py:80
  531.7 1.7 reshape.38
  533.4 3.0 convolution_convert_fusion.1
  (28 shorter events, 1.6 us)
Async XLA Ops:
  6.5 2.5 copy-start
  6.5 8.4 %copy-start.6 = (bf16[16,3584]{1,0:T(8,128)(2,1)S(1)}, bf16[16,3584]{1,0:T(8,128)(2,1)}, u32[]{:S(2)}) copy-start(bf16[16,3584]{1,0:T(8,128)(2,1)} %param.7) | copy-start | bytes 344068
  6.5 464.9 %all-reduce.3.cloned.1.call-start = ((), (), s32[]{:S(2)}) async-start(), calls=%async_computation.3 | async-start | bytes 14680064
  293.1 2.6 copy-start.2
  298.8 5.3 copy-start.3
  307.9 7.4 %copy-start.4 = (f32[4,64,2,2,256]{4,1,3,0,2:T(8,128)S(1)}, f32[4,64,2,2,256]{4,1,3,0,2:T(8,128)}, u32[]{:S(2)}) copy-start(f32[4,64,2,2,256]{4,1,3,0,2:T(8,128)} %fusion.14) | copy-start | bytes 3145732
  307.9 7.3 %copy-start.5 = (f32[4,64,2,2,256]{4,1,3,0,2:T(8,128)S(1)}, f32[4,64,2,2,256]{4,1,3,0,2:T(8,128)}, u32[]{:S(2)}) copy-start(f32[4,64,2,2,256]{4,1,3,0,2:T(8,128)} %fusion.17) | copy-start | bytes 3145732
  326.6 0.7 copy-start.7
  475.6 60.7 %copy-start.1 = (bf16[16,3584]{1,0:T(8,128)(2,1)S(1)}, bf16[16,3584]{1,0:T(8,128)(2,1)}, u32[]{:S(2)}) copy-start(bf16[16,3584]{1,0:T(8,128)(2,1)} %param.8) | copy-start | bytes 344068
Sparse Core Ops, SparseCore 0:
  326.7 144.6 all-reduce.2
